TPU v7x, 32 devices: a whole 2x2x4 slice. The times are simulated.
32 devices in a mesh: ep: 32 (over z, y, x, core).
Axes of the slice: x: 2, y: 2, z: 4, core: 2. Of those that a mesh axis runs over, the one named last changes fastest.
Arguments:
- hidden: bfloat16 [32768, 1536], P('ep')
- grad_out: bfloat16 [32768, 1536], P('ep')
- w_router: bfloat16 [1536, 64], replicated
- b_router: float32 [64], replicated
- expert_ids: int32 [32768, 6], P('ep')
- slot_ids: int32 [32768, 6], P('ep')
- w_gate_up: bfloat16 [64, 1536, 1024], P('ep')
- b_gate_up: float32 [64, 1024], P('ep')
- w_down: bfloat16 [64, 512, 1536], P('ep')
- b_down: float32 [64, 1536], P('ep')
Outputs:
- output 1: bfloat16 [32768, 1536], P('ep')
- output 2: bfloat16 [32768, 1536], P('ep')
- output 3: float32 [1536, 64], replicated
- output 4: float32 [64], replicated
- output 5: float32 [64, 1536, 1024], P('ep')
- output 6: float32 [64, 1024], P('ep')
- output 7: float32 [64, 512, 1536], P('ep')
- output 8: float32 [64, 1536], P('ep')
All inputs are finite; a program needn't handle non-finite values.
Results may differ from a plain program's by a relative error of at most 0.00506232.
Values are sent between devices in bfloat16 or wider.
A program may use at most 1 GiB of HBM per device.

v0:
```python
import jax
import jax.numpy as jnp
from jax import lax
from jax.sharding import PartitionSpec as P

SWIGLU_LIMIT = 7.0
SWIGLU_ALPHA = 1.702


def swiglu(pre_act):
    col_pairs = pre_act.reshape(pre_act.shape[:-1] + (pre_act.shape[-1] // 2, 2))
    gate_in = jnp.minimum(col_pairs[..., 0], SWIGLU_LIMIT)
    up_in = jnp.clip(col_pairs[..., 1], -SWIGLU_LIMIT, SWIGLU_LIMIT)
    return gate_in * jax.nn.sigmoid(SWIGLU_ALPHA * gate_in) * (up_in + 1.0)


def solution(mesh):
    ep_size = mesh.shape['ep']

    def local_block(hidden, grad_out, w_router, b_router, expert_ids, slot_ids, w_gate_up, b_gate_up, w_down, b_down):
        tok_local, d_model = hidden.shape
        top_k = expert_ids.shape[1]
        experts = w_router.shape[1]
        local_experts = w_gate_up.shape[0]
        capacity = (3 * tok_local * top_k + 2 * experts - 1) // (2 * experts)
        buf_rows = experts * capacity
        copy_count = tok_local * top_k
        dest_row = jnp.where(slot_ids >= 0, expert_ids * capacity + slot_ids, buf_rows)
        src_copy = jnp.full((buf_rows + 1,), copy_count, jnp.int32).at[dest_row.reshape(-1)].set(jnp.arange(copy_count, dtype=jnp.int32))[:buf_rows]
        src_tok = src_copy // top_k
        logits = jnp.dot(hidden, w_router, preferred_element_type=jnp.float32) + b_router
        gate_w = jax.nn.softmax(jnp.take_along_axis(logits, expert_ids, axis=1), axis=-1)

        send_x = jnp.take(hidden, src_tok, axis=0, mode='fill', fill_value=0)
        recv_x = lax.all_to_all(send_x, 'ep', 0, 0, tiled=True).reshape(ep_size, local_experts, capacity, d_model)
        pre_act = jnp.einsum('secd,edf->secf', recv_x, w_gate_up, preferred_element_type=jnp.float32) + b_gate_up[None, :, None, :]
        act_val, act_vjp = jax.vjp(swiglu, pre_act)
        act_bf = act_val.astype(jnp.bfloat16)
        y_rows = (jnp.einsum('secf,efd->secd', act_bf, w_down, preferred_element_type=jnp.float32) + b_down[None, :, None, :]).astype(jnp.bfloat16)
        back_y = lax.all_to_all(y_rows.reshape(buf_rows, d_model), 'ep', 0, 0, tiled=True)
        y_copies = jnp.take(back_y, dest_row, axis=0, mode='fill', fill_value=0)
        block_out = jnp.sum(gate_w[:, :, None] * y_copies, axis=1).astype(jnp.bfloat16)

        gate_grad = jnp.einsum('td,tkd->tk', grad_out, y_copies, preferred_element_type=jnp.float32)
        sel_grad = gate_w * (gate_grad - jnp.sum(gate_w * gate_grad, axis=1, keepdims=True))
        expert_range = jnp.arange(experts, dtype=jnp.int32)
        logit_grad = jnp.sum(jnp.where(expert_ids[:, :, None] == expert_range, sel_grad[:, :, None], 0.0), axis=1).astype(jnp.bfloat16)
        row_gate = jnp.take(gate_w.reshape(-1), src_copy, axis=0, mode='fill', fill_value=0)
        row_grad = jnp.take(grad_out, src_tok, axis=0, mode='fill', fill_value=0)
        send_q = (row_gate[:, None] * row_grad).astype(jnp.bfloat16)
        recv_q = lax.all_to_all(send_q, 'ep', 0, 0, tiled=True).reshape(ep_size, local_experts, capacity, d_model)
        grad_b_down = jnp.sum(recv_q, axis=(0, 2), dtype=jnp.float32)
        grad_w_down = jnp.einsum('secf,secd->efd', act_bf, recv_q, preferred_element_type=jnp.float32)
        act_grad = jnp.einsum('secd,efd->secf', recv_q, w_down, preferred_element_type=jnp.float32)
        pre_grad = act_vjp(act_grad)[0].astype(jnp.bfloat16)
        grad_b_gate_up = jnp.sum(pre_grad, axis=(0, 2), dtype=jnp.float32)
        grad_w_gate_up = jnp.einsum('secd,secf->edf', recv_x, pre_grad, preferred_element_type=jnp.float32)
        p_rows = jnp.einsum('secf,edf->secd', pre_grad, w_gate_up, preferred_element_type=jnp.float32).astype(jnp.bfloat16)
        back_p = lax.all_to_all(p_rows.reshape(buf_rows, d_model), 'ep', 0, 0, tiled=True)
        p_copies = jnp.take(back_p, dest_row, axis=0, mode='fill', fill_value=0)
        router_dx = jnp.einsum('te,de->td', logit_grad, w_router, preferred_element_type=jnp.float32)
        grad_hidden = (jnp.sum(p_copies, axis=1, dtype=jnp.float32) + router_dx).astype(jnp.bfloat16)
        grad_w_router = lax.psum(jnp.einsum('td,te->de', hidden, logit_grad, preferred_element_type=jnp.float32), 'ep')
        grad_b_router = lax.psum(jnp.sum(logit_grad, axis=0, dtype=jnp.float32), 'ep')
        return (block_out, grad_hidden, grad_w_router, grad_b_router, grad_w_gate_up, grad_b_gate_up, grad_w_down, grad_b_down)

    tok_spec = P('ep', None)
    in_specs = (tok_spec, tok_spec, P(None, None), P(None), tok_spec, tok_spec, P('ep', None, None), P('ep', None), P('ep', None, None), P('ep', None))
    out_specs = (tok_spec, tok_spec, P(None, None), P(None), P('ep', None, None), P('ep', None), P('ep', None, None), P('ep', None))
    return jax.shard_map(local_block, mesh=mesh, in_specs=in_specs, out_specs=out_specs, check_vma=False)
```

profile of v0, /device:TPU:0, one launch (start us, length us, event | category | flops | bytes accessed | tf_op | source)
XLA Modules:
  0.0 3576.4 jit_solution(650246981336762577)
XLA Ops:
  7.2 1.5 compare_and_fusion.1
  9.8 1.4 reshape.174
  11.2 23.0 scatter_custom_fusion
  35.0 57.7 %gather_fusion.2 = bf16[9216,1536]{1,0:T(8,128)(2,1)} fusion(bf16[1024,1536]{1,0:T(8,128)(2,1)} %param.14, s32[9216]{0:T(1024)S(1)} %get-tuple-element.23), kind=kCustom, calls=%fused_computation.clone | custom fusion | bytes 56659968 | tf_op jit(solution)/shard_map/jit(_take)/gather | solution.py:34
  92.6 19.7 broadcast_select_fusion
  112.3 629.8 %all_to_all.42 = bf16[32,288,1536]{2,1,0:T(8,128)(2,1)} all-to-all(bf16[32,288,1536]{2,1,0:T(8,128)(2,1)} %bitcast.118), channel_id=1, replica_groups=mesh['ep'=32] {'ep'}, dimensions={0} | all-to-all | bytes 56623104 | tf_op jit(solution)/shard_map/all_to_all | solution.py:35
  742.1 36.1 %add_bitcast_fusion = f32[32,2,144,1024]{3,2,0,1:T(8,128)} fusion(bf16[32,2,144,1536]{3,2,1,0:T(8,128)(2,1)} %bitcast.121, f32[2,1024]{1,0:T(2,128)S(1)} %copy-done.30, bf16[2,1536,1024]{2,1,0:T(8,128)(2,1)S(1)} %copy-done.28), kind=kOutput, calls=%fused_computation.14 | convolution fusion | flops 29000466432 | bytes 72359936 | tf_op jit(solution)/shard_map/secd,edf->secf/dot_general | solution.py:36
  778.3 69.0 %copy.100 = f32[32,2,144,1024]{2,0,3,1:T(8,128)} copy(f32[32,2,144,1024]{3,2,0,1:T(8,128)} %add_bitcast_fusion) | data formatting | bytes 75497472 | tf_op jit(solution)/shard_map/add | solution.py:36
  847.3 43.8 %fusion.52 = (f32[32,2,144,512,1]{2,0,4,3,1:T(8,128)}, f32[32,2,144,512,1]{2,0,4,3,1:T(8,128)}) fusion(f32[32,2,144,512,2]{2,0,4,3,1:T(8,128)} %bitcast.7), kind=kLoop, calls=%fused_computation.96 | loop fusion | bytes 75497472 | tf_op jit(solution)/shard_map/jvp()/slice | solution.py:12
  891.1 31.4 copy.121
  922.5 31.4 copy.120
  953.9 17.4 fusion.22
  971.4 21.9 fusion.13
  993.2 19.4 copy.103
  1012.7 4.5 all-to-all-start.1
  1017.2 57.7 %gather_fusion.4 = bf16[9216,1536]{1,0:T(8,128)(2,1)} fusion(bf16[1024,1536]{1,0:T(8,128)(2,1)} %param.15, s32[9216]{0:T(1024)S(1)} %copy-done.14), kind=kCustom, calls=%fused_computation.2.clone | custom fusion | bytes 56659968 | tf_op jit(solution)/shard_map/jit(_take)/gather | solution.py:49
  1075.9 2.0 reshape.246
  1079.9 1.4 reshape.218
  1081.2 3.0 convolution_add_fusion
  1084.2 49.3 %gather_fusion.1 = f32[6144]{0:T(1024)S(1)} fusion(f32[1024,64]{0,1:T(8,128)S(1)} %convolution_add_fusion, s32[6144]{0:T(1024)S(1)} %reshape.218), kind=kCustom, calls=%fused_computation.5 | custom fusion | bytes 98304 | tf_op jit(solution)/shard_map/jit(take_along_axis)/gather | solution.py:32
  1133.5 1.3 reshape.221
  1134.8 1.2 copy.95
  1136.1 465.3 %all-to-all-done.1 = bf16[32,288,1536]{2,1,0:T(8,128)(2,1)} async-done(((bf16[32,288,1536]{2,1,0:T(8,128)(2,1)}), bf16[32,288,1536]{2,1,0:T(8,128)(2,1)}, u32[]{:S(2)}, u32[]{:S(2)}) %all-to-all-start.1) | async-done | bytes 28311584 | tf_op jit(solution)/shard_map/all_to_all | solution.py:40
  1601.4 50.0 %gather_fusion.3 = bf16[6144,1536]{1,0:T(8,128)(2,1)} fusion(bf16[9216,1536]{1,0:T(8,128)(2,1)} %bitcast.14, s32[6144]{0:T(1024)S(1)} %broadcast_clamp_fusion.1), kind=kCustom, calls=%fused_computation.1.clone | custom fusion | bytes 37773312 | tf_op jit(solution)/shard_map/jit(_take)/gather | solution.py:41
  1651.5 29.2 reshape.249
  1680.7 19.4 fusion.12
  1702.9 1.4 div.27
  1704.3 51.4 %gather_fusion = f32[9216]{0:T(1024)S(1)} fusion(f32[6144]{0:T(1024)S(1)} %div.27, s32[9216]{0:T(1024)S(1)} %copy-done.21), kind=kCustom, calls=%fused_computation.4 | custom fusion | bytes 110592 | tf_op jit(solution)/shard_map/jit(_take)/gather | solution.py:48
  1755.8 19.9 multiply_convert_fusion
  1775.6 654.1 %all_to_all.43 = bf16[32,288,1536]{2,1,0:T(8,128)(2,1)} all-to-all(bf16[32,288,1536]{2,1,0:T(8,128)(2,1)} %bitcast.117), channel_id=1, replica_groups=mesh['ep'=32] {'ep'}, dimensions={0} | all-to-all | bytes 56623104 | tf_op jit(solution)/shard_map/all_to_all | solution.py:51
  2429.7 43.1 %fusion.21 = (f32[32,2,144,512,1]{3,2,0,1,4:T(8,128)}, f32[32,2,144,512,1]{3,2,0,1,4:T(8,128)}) fusion(f32[32,2,144,512,1]{3,2,0,1,4:T(8,128)} %copy.121, f32[32,2,144,512,1]{3,2,0,1,4:T(8,128)} %copy.120, bf16[2,512,1536]{2,1,0:T(8,128)(2,1)S(1)} %copy-done, bf16[32,2,144,1536]{3,2,1,0:T(8,128)(2,1)} %bitcast.113), kind=kOutput, calls=%fused_computation.37 | convolution fusion | flops 14651228160 | bytes 106954752 | tf_op jit(solution)/shard_map/secd,efd->secf/dot_general | solution.py:54
  2472.8 21.8 convert_reduce_fusion.2
  2494.7 51.7 %copy.108 = bf16[32,2,144,512,2]{2,0,4,3,1:T(8,128)(2,1)} copy(bf16[32,2,144,512,2]{3,2,0,1,4:T(8,128)(2,1)} %get-tuple-element.13) | data formatting | bytes 37748736 | tf_op jit(solution)/shard_map/convert_element_type | solution.py:55
  2546.3 65.3 %convert_bitcast_fusion = bf16[32,2,144,1536]{3,2,0,1:T(8,128)(2,1)} fusion(bf16[32,2,144,1024]{2,0,3,1:T(8,128)(2,1)} %bitcast.119, bf16[2,1536,1024]{2,1,0:T(8,128)(2,1)} %param.20), kind=kOutput, calls=%fused_computation.21 | convolution fusion | flops 29005185024 | bytes 53477376 | tf_op jit(solution)/shard_map/secf,edf->secd/dot_general | solution.py:58
  2611.7 19.4 copy.110
  2631.1 14.1 all-to-all-start.3
  2645.5 3.3 convolution_bitcast_fusion
  2649.0 643.7 %psum.15 = f32[64]{0:T(128)} all-reduce(f32[64]{0:T(128)S(1)} %convert_reduce_fusion.3), channel_id=1, replica_groups=mesh['ep'=32] {'ep'}, use_global_device_ids=true, to_apply=%region_9.12 | all-reduce | flops 64 | bytes 512 | tf_op jit(solution)/shard_map/psum | solution.py:64
  3293.7 2.0 reduce_sum.88
  3295.7 11.5 convert_reduce_fusion
  3307.2 2.2 reduce_sum.91
  3309.4 22.7 fusion.34
  3332.1 77.5 %fusion.28 = f32[2,1536,1024]{2,1,0:T(8,128)} fusion(bf16[32,2,144,1536]{3,2,1,0:T(8,128)(2,1)} %bitcast.122, bf16[32,2,144,1024]{2,0,3,1:T(8,128)(2,1)} %bitcast.120), kind=kOutput, calls=%fused_computation.52 | convolution fusion | flops 28991029248 | bytes 59768832 | tf_op jit(solution)/shard_map/secd,secf->edf/dot_general | solution.py:57
  3409.6 50.0 %gather_fusion.5 = bf16[6144,1536]{1,0:T(8,128)(2,1)} fusion(bf16[9216,1536]{1,0:T(8,128)(2,1)} %bitcast.28, s32[6144]{0:T(1024)S(1)} %copy-done.2), kind=kCustom, calls=%fused_computation.3.clone | custom fusion | bytes 37773312 | tf_op jit(solution)/shard_map/jit(_take)/gather | solution.py:60
  3459.6 29.3 reshape.255
  3488.9 76.0 %convert_reduce_fusion.1 = (f32[1024,1536]{1,0:T(8,128)S(1)}, bf16[1024,1536]{1,0:T(8,128)(2,1)}) fusion(bf16[1024,6,1536]{2,1,0:T(8,128)(2,1)} %reshape.255, pred[1024,6]{1,0:T(8,128)(4,1)S(1)} %copy-done.12, bf16[1024,6,1536]{2,1,0:T(8,128)(2,1)} %reshape.249, f32[1024,6]{1,0:T(8,128)} %copy.96), kind=kLoop, calls=%fused_computation.10 | loop fusion | flops 62914560 | bytes 47216640 | tf_op jit(solution)/shard_map/reduce_sum | solution.py:62
  3564.9 2.7 add_convert_fusion.2
  3567.6 1.8 copy.145
  (87 shorter events, 9.2 us)
Async XLA Ops:
  7.2 964.2 %copy-start = (bf16[2,512,1536]{2,1,0:T(8,128)(2,1)S(1)}, bf16[2,512,1536]{2,1,0:T(8,128)(2,1)}, u32[]{:S(2)}) copy-start(bf16[2,512,1536]{2,1,0:T(8,128)(2,1)} %param.22) | copy-start | bytes 9437188
  8.7 2.5 copy-start.17
  34.2 58.4 %copy-start.9 = (s32[9217]{0:T(1024)}, s32[9217]{0:T(1024)S(1)}, u32[]{:S(2)}) copy-start(s32[9217]{0:T(1024)S(1)} %scatter_custom_fusion) | copy-start | bytes 110608
  34.9 57.7 %copy-start.13 = (s32[9216]{0:T(1024)}, s32[9216]{0:T(1024)S(1)}, u32[]{:S(2)}) copy-start(s32[9216]{0:T(1024)S(1)} %get-tuple-element.23) | copy-start | bytes 110596
  34.9 57.7 %copy-start.23 = (pred[9216]{0:T(1024)(128)(4,1)}, pred[9216]{0:T(1024)(128)(4,1)S(1)}, u32[]{:S(2)}) copy-start(pred[9216]{0:T(1024)(128)(4,1)S(1)} %compare_and_fusion) | copy-start | bytes 27652
  112.3 629.8 %copy-start.28 = (bf16[2,1536,1024]{2,1,0:T(8,128)(2,1)S(1)}, bf16[2,1536,1024]{2,1,0:T(8,128)(2,1)}, u32[]{:S(2)}) copy-start(bf16[2,1536,1024]{2,1,0:T(8,128)(2,1)} %param.20) | copy-start | bytes 18874372
  112.3 629.8 %copy-start.30 = (f32[2,1024]{1,0:T(2,128)S(1)}, f32[2,1024]{1,0:T(2,128)}, u32[]{:S(2)}) copy-start(f32[2,1024]{1,0:T(2,128)} %param.21) | copy-start | bytes 24580
  953.9 17.4 copy-start.29
  1012.7 4.5 copy-start.14
  1012.7 588.8 %all-to-all-start.1 = ((bf16[32,288,1536]{2,1,0:T(8,128)(2,1)}), bf16[32,288,1536]{2,1,0:T(8,128)(2,1)}, u32[]{:S(2)}, u32[]{:S(2)}) async-start(bf16[32,288,1536]{2,1,0:T(8,128)(2,1)} %bitcast.116), calls=%async_computation.1 | async-start | bytes 56623104 | tf_op jit(solution)/shard_map/all_to_all | solution.py:40
  1017.2 57.7 %copy-start.18 = (s32[1024,6]{0,1:T(8,128)S(1)}, s32[1024,6]{0,1:T(8,128)}, u32[]{:S(2)}) copy-start(s32[1024,6]{0,1:T(8,128)} %copy-done.17) | copy-start | bytes 73732
  1017.2 60.7 %copy-start.25 = (pred[1024,6]{0,1:T(8,128)(4,1)S(1)}, pred[1024,6]{0,1:T(8,128)(4,1)}, u32[]{:S(2)}) copy-start(pred[1024,6]{0,1:T(8,128)(4,1)} %get-tuple-element.16) | copy-start | bytes 18436
  1017.2 61.6 %copy-start.5 = (s32[1024,6]{0,1:T(8,128)S(1)}, s32[1024,6]{0,1:T(8,128)}, u32[]{:S(2)}) copy-start(s32[1024,6]{0,1:T(8,128)} %param.18) | copy-start | bytes 73732
  1017.2 64.0 %copy-start.27 = (f32[64]{0:T(128)S(1)}, f32[64]{0:T(128)}, u32[]{:S(2)}) copy-start(f32[64]{0:T(128)} %param.17) | copy-start | bytes 772
  1084.2 51.8 %copy-start.6 = (s32[1024,6]{0,1:T(8,128)S(1)}, s32[1024,6]{0,1:T(8,128)}, u32[]{:S(2)}) copy-start(s32[1024,6]{0,1:T(8,128)} %param.18) | copy-start | bytes 73732
  1084.2 51.9 %copy-start.22 = (s32[6144]{0:T(1024)S(1)}, s32[6144]{0:T(1024)}, u32[]{:S(2)}) copy-start(s32[6144]{0:T(1024)} %reshape.246) | copy-start | bytes 73732
  1136.1 515.4 %copy-start.1 = (s32[6144]{0:T(1024)}, s32[6144]{0:T(1024)S(1)}, u32[]{:S(2)}) copy-start(s32[6144]{0:T(1024)S(1)} %broadcast_clamp_fusion.1) | copy-start | bytes 73732
  1651.5 29.2 copy-start.11
  1680.7 23.6 copy-start.21
  1701.3 54.5 %copy-start.15 = (f32[1024,1,6]{0,2,1:T(8,128)}, f32[1024,1,6]{0,2,1:T(8,128)S(1)}, u32[]{:S(2)}) copy-start(f32[1024,1,6]{0,2,1:T(8,128)S(1)} %copy.118) | copy-start | bytes 73732
  1701.9 53.8 %copy-start.19 = (f32[1024,6]{0,1:T(8,128)}, f32[1024,6]{0,1:T(8,128)S(1)}, u32[]{:S(2)}) copy-start(f32[1024,6]{0,1:T(8,128)S(1)} %get-tuple-element.15) | copy-start | bytes 73732
  1704.3 51.4 %copy-start.10 = (s32[9217]{0:T(1024)S(1)}, s32[9217]{0:T(1024)}, u32[]{:S(2)}) copy-start(s32[9217]{0:T(1024)} %copy-done.9) | copy-start | bytes 110608
  1704.3 51.4 %copy-start.24 = (pred[9216]{0:T(1024)(128)(4,1)S(1)}, pred[9216]{0:T(1024)(128)(4,1)}, u32[]{:S(2)}) copy-start(pred[9216]{0:T(1024)(128)(4,1)} %copy-done.23) | copy-start | bytes 27652
  2631.1 14.2 copy-start.16
  2631.1 14.2 copy-start.20
  2631.1 14.2 copy-start.26
  2631.1 14.2 copy-start.7
  2631.1 778.5 %all-to-all-start.3 = ((bf16[32,288,1536]{2,1,0:T(8,128)(2,1)}), bf16[32,288,1536]{2,1,0:T(8,128)(2,1)}, u32[]{:S(2)}, u32[]{:S(2)}) async-start(bf16[32,288,1536]{2,1,0:T(8,128)(2,1)} %bitcast.115), calls=%async_computation.3 | async-start | bytes 56623104 | tf_op jit(solution)/shard_map/all_to_all | solution.py:59
  2645.2 922.3 %all-reduce.4.cloned.1.call-start = ((), (), s32[]{:S(2)}) async-start(), calls=%async_computation.4 | async-start | bytes 786432 | tf_op jit(solution)/shard_map/psum | solution.py:63
  2645.5 663.9 %copy-start.3 = (bf16[1024,64]{0,1:T(8,128)(2,1)}, bf16[1024,64]{0,1:T(8,128)(2,1)S(1)}, u32[]{:S(2)}) copy-start(bf16[1024,64]{0,1:T(8,128)(2,1)S(1)} %select_reduce_fusion) | copy-start | bytes 393220
  3332.1 77.5 %copy-start.2 = (s32[6144]{0:T(1024)S(1)}, s32[6144]{0:T(1024)}, u32[]{:S(2)}) copy-start(s32[6144]{0:T(1024)} %copy-done.1) | copy-start | bytes 73732
  3459.6 29.3 copy-start.12
  3488.9 76.0 %copy-start.4 = (bf16[1024,64]{0,1:T(8,128)(2,1)S(1)}, bf16[1024,64]{0,1:T(8,128)(2,1)}, u32[]{:S(2)}) copy-start(bf16[1024,64]{0,1:T(8,128)(2,1)} %copy-done.3) | copy-start | bytes 393220
  3488.9 76.0 %copy-start.8 = (bf16[1536,64]{0,1:T(8,128)(2,1)S(1)}, bf16[1536,64]{0,1:T(8,128)(2,1)}, u32[]{:S(2)}) copy-start(bf16[1536,64]{0,1:T(8,128)(2,1)} %param.16) | copy-start | bytes 589828
Sparse Core Ops, SparseCore 0:
  2651.9 357.5 all-reduce.3
where the time goes:
time: 3580 us
  blocking collectives  1930 us (54%)
  local copies, waits for them, and re-layouts  683 us (19%)
  waiting for transfers between devices  465 us (13%)
  matrix products  295 us (8%)
  other arithmetic  172 us (5%)
    all_to_all x1, blocking collectives, local_block(): lax.all_to_all(send_q, 'ep', 0, 0, tiled=True)  654 us
    psum x1, blocking collectives, local_block(): lax.psum(jnp.sum(logit_grad, axis=0, dtype=jnp.float32), 'ep')  644 us
    all_to_all x1, blocking collectives, local_block(): lax.all_to_all(send_x, 'ep', 0, 0, tiled=True)  630 us
    all_to_all x1, waiting for transfers between devices, local_block(): lax.all_to_all(y_rows.reshape(buf_rows, d_model), 'ep', 0, 0, tiled=True)  465 us
    gather x2, local copies, waits for them, and re-layouts, local_block(): p_copies = jnp.take(back_p, dest_row, axis=0, mode='fill', fill_value=0)  79.3 us
    gather x2, local copies, waits for them, and re-layouts, local_block(): y_copies = jnp.take(back_y, dest_row, axis=0, mode='fill', fill_value=0)  79.3 us
    dot_general x1, matrix products, local_block(): jnp.einsum('secd,secf->edf', recv_x, pre_grad, preferred_element_type=jnp...  77.5 us
    reduce_sum x1, other arithmetic, local_block(): jnp.sum(p_copies, axis=1, dtype=jnp.float32) + router_dx  76 us
  transfers between devices with their start and end apart: 3, of which 1 were waited for; matrix products, arithmetic and copies ran while one was open for 11% of the time, Pallas kernels for 0%

commit v1 on v0

v1 whole, which is shorter than its diff:
```python
import jax
import jax.numpy as jnp
from jax import lax
from jax.sharding import PartitionSpec as P

SWIGLU_LIMIT = 7.0
SWIGLU_ALPHA = 1.702


def gated_act(gate_pre, up_pre):
    gate_in = jnp.minimum(gate_pre, SWIGLU_LIMIT)
    up_in = jnp.clip(up_pre, -SWIGLU_LIMIT, SWIGLU_LIMIT)
    return gate_in * jax.nn.sigmoid(SWIGLU_ALPHA * gate_in) * (up_in + 1.0)


def take_rows(rows, index):
    return rows.at[index].get(mode='promise_in_bounds')


def solution(mesh):
    ep_size = mesh.shape['ep']

    def local_block(hidden, grad_out, w_router, b_router, expert_ids, slot_ids, w_gate_up, b_gate_up, w_down, b_down):
        f32, bf16 = jnp.float32, jnp.bfloat16
        tok_local, d_model = hidden.shape
        top_k = expert_ids.shape[1]
        experts = w_router.shape[1]
        local_experts = w_gate_up.shape[0]
        ff = w_down.shape[1]
        capacity = (3 * tok_local * top_k + 2 * experts - 1) // (2 * experts)
        part_rows = ep_size * capacity
        buf_rows = experts * capacity
        copy_count = tok_local * top_k

        ids_t, slots_t = expert_ids.T, slot_ids.T
        kept = slots_t >= 0
        row_t = (ids_t % local_experts) * part_rows + (ids_t // local_experts) * capacity + slots_t
        dest_row = jnp.where(kept, row_t, buf_rows)
        src_copy = jnp.full((buf_rows + 1,), copy_count, jnp.int32).at[dest_row.reshape(-1)].set(jnp.arange(copy_count, dtype=jnp.int32))[:buf_rows]
        src_tok = jnp.where(src_copy < copy_count, src_copy % tok_local, tok_local)
        back_row = jnp.where(kept, row_t, 0).reshape(-1)

        def exchange(rows):
            return lax.all_to_all(rows, 'ep', 0, 0, tiled=True)

        def part(index, e):
            return lax.slice(index, (e * part_rows,), ((e + 1) * part_rows,))

        hidden_pad = jnp.pad(hidden, ((0, 16), (0, 0)))
        recv_x = [exchange(take_rows(hidden_pad, part(src_tok, e))) for e in range(local_experts)]

        logits = jnp.dot(hidden, w_router, preferred_element_type=f32) + b_router
        expert_range = jnp.arange(experts, dtype=jnp.int32)
        chosen = ids_t[:, :, None] == expert_range
        gate_w = jax.nn.softmax(jnp.sum(jnp.where(chosen, logits[None], 0.0), axis=2), axis=0)
        q_copies = (gate_w[:, :, None] * grad_out[None].astype(f32)).astype(bf16).reshape(copy_count, d_model)
        q_copies = jnp.pad(q_copies, ((0, 16), (0, 0)))

        col = jnp.arange(2 * ff, dtype=jnp.int32)
        split = (col[:, None] == jnp.where(col < ff, 2 * col, 2 * (col - ff) + 1)[None, :]).astype(bf16)
        w_split = [jnp.dot(w_gate_up[e], split, preferred_element_type=f32).astype(bf16) for e in range(local_experts)]

        acts, vjps, back_y = [], [], []
        for e in range(local_experts):
            b_pair = b_gate_up[e].reshape(ff, 2)
            b_split = jnp.concatenate([b_pair[:, 0], b_pair[:, 1]])
            pre_act = jnp.dot(recv_x[e], w_split[e], preferred_element_type=f32) + b_split
            act_val, act_vjp = jax.vjp(gated_act, pre_act[:, :ff], pre_act[:, ff:])
            act_bf = act_val.astype(bf16)
            y_rows = (jnp.dot(act_bf, w_down[e], preferred_element_type=f32) + b_down[e]).astype(bf16)
            acts.append(act_bf)
            vjps.append(act_vjp)
            back_y.append(exchange(y_rows))

        recv_q = [exchange(take_rows(q_copies, part(src_copy, e))) for e in range(local_experts)]

        y_copies = take_rows(jnp.concatenate(back_y), back_row).reshape(top_k, tok_local, d_model)
        y_kept = jnp.where(kept[:, :, None], y_copies, 0).astype(f32)
        block_out = jnp.sum(gate_w[:, :, None] * y_kept, axis=0).astype(bf16)
        gate_grad = jnp.sum(grad_out[None].astype(f32) * y_kept, axis=2)
        sel_grad = gate_w * (gate_grad - jnp.sum(gate_w * gate_grad, axis=0, keepdims=True))
        logit_grad = jnp.sum(jnp.where(chosen, sel_grad[:, :, None], 0.0), axis=0).astype(bf16)
        grad_w_router = lax.psum(jnp.dot(hidden.T, logit_grad, preferred_element_type=f32), 'ep')
        grad_b_router = lax.psum(jnp.sum(logit_grad, axis=0, dtype=f32), 'ep')
        router_dx = jnp.dot(logit_grad, w_router.T, preferred_element_type=f32)

        back_p, pre_grads = [], []
        for e in range(local_experts):
            act_grad = jnp.dot(recv_q[e], w_down[e].T, preferred_element_type=f32)
            gate_d, up_d = vjps[e](act_grad)
            pre_split = jnp.concatenate([gate_d.astype(bf16), up_d.astype(bf16)], axis=1)
            if e == local_experts - 1:
                pre_split, _ = lax.optimization_barrier((pre_split, (logit_grad, block_out)))
            p_rows = jnp.dot(pre_split, w_split[e].T, preferred_element_type=f32).astype(bf16)
            back_p.append(exchange(p_rows))
            pre_grads.append(pre_split)

        g_wd, g_bd, g_wgu, g_bgu = [], [], [], []
        for e in range(local_experts):
            pre_grad = jnp.dot(pre_grads[e], split.T, preferred_element_type=f32).astype(bf16)
            g_bd.append(jnp.sum(recv_q[e], axis=0, dtype=f32))
            g_wd.append(jnp.dot(acts[e].T, recv_q[e], preferred_element_type=f32))
            g_bgu.append(jnp.sum(pre_grad, axis=0, dtype=f32))
            g_wgu.append(jnp.dot(recv_x[e].T, pre_grad, preferred_element_type=f32))

        dx = router_dx
        for e in range(local_experts):
            here = kept & (ids_t % local_experts == e)
            row_e = jnp.where(here, row_t - e * part_rows, 0).reshape(-1)
            p_copies = take_rows(back_p[e], row_e).reshape(top_k, tok_local, d_model)
            dx = dx + jnp.sum(jnp.where(here[:, :, None], p_copies, 0).astype(f32), axis=0)
        grad_hidden = dx.astype(bf16)
        return (block_out, grad_hidden, grad_w_router, grad_b_router, jnp.stack(g_wgu), jnp.stack(g_bgu), jnp.stack(g_wd), jnp.stack(g_bd))

    tok_spec = P('ep', None)
    in_specs = (tok_spec, tok_spec, P(None, None), P(None), tok_spec, tok_spec, P('ep', None, None), P('ep', None), P('ep', None, None), P('ep', None))
    out_specs = (tok_spec, tok_spec, P(None, None), P(None), P('ep', None, None), P('ep', None), P('ep', None, None), P('ep', None))
    return jax.shard_map(local_block, mesh=mesh, in_specs=in_specs, out_specs=out_specs, check_vma=False)
```

time: 3580 us -> 2730 us (0.76)
  blocking collectives: 1930 us -> 209 us
  waiting for transfers between devices: 465 us -> 1690 us
  local copies, waits for them, and re-layouts: 683 us -> 286 us
  starting transfers between devices: 18.6 us -> 130 us
  other arithmetic: 172 us -> 130 us
    all_to_all x2 -> x0, blocking collectives: 1280 us -> none  [the longest x1 654 us: local_block(): lax.all_to_all(send_q, 'ep', 0, 0, tiled=True)]
    all_to_all x2 -> x8, waiting for transfers between devices: 465 us -> 1690 us  [exchange(): return lax.all_to_all(rows, 'ep', 0, 0, tiled=True)]
    psum x1, blocking collectives: 644 us -> 209 us  [local_block(): grad_b_router = lax.psum(jnp.sum(logit_grad, axis=0, dtype=f32), 'ep')]
    gather x12 -> x7, local copies, waits for them, and re-layouts: 379 us -> 245 us  [take_rows(): return rows.at[index].get(mode='promise_in_bounds')]
    all_to_all x2 -> x8, starting transfers between devices: 18.6 us -> 130 us  [exchange(): return lax.all_to_all(rows, 'ep', 0, 0, tiled=True)]
    convert_element_type x3 -> x0, local copies, waits for them, and re-layouts: 90.5 us -> none  [the longest x1 51.7 us: local_block(): pre_grad = act_vjp(act_grad)[0].astype(jnp.bfloat16)]
    add x1 -> x0, local copies, waits for them, and re-layouts: 69 us -> none  [local_block(): jnp.einsum('secd,edf->secf', recv_x, w_gate_up, preferred_element_type=jn...]
    unnamed x65 -> x83, local copies, waits for them, and re-layouts: 64.7 us -> 6.45 us
  transfers between devices with their start and end apart: 3 -> 9, of which waited for: 1 -> 7; matrix products, arithmetic and copies ran while one was open for 11% -> 23% of each run, Pallas kernels for 0% -> 0%
where the time goes in v1:
time: 2730 us; the launch traced here: 2720 us
  waiting for transfers between devices  1690 us (62%)
  local copies, waits for them, and re-layouts  286 us (10%)
  matrix products  260 us (10%)
  blocking collectives  209 us (8%)
  other arithmetic  130 us (5%)
  starting transfers between devices  130 us (5%)
    all_to_all x8, waiting for transfers between devices, exchange(): return lax.all_to_all(rows, 'ep', 0, 0, tiled=True)  1690 us
    gather x7, local copies, waits for them, and re-layouts, take_rows(): return rows.at[index].get(mode='promise_in_bounds')  245 us
    psum x1, blocking collectives, local_block(): grad_b_router = lax.psum(jnp.sum(logit_grad, axis=0, dtype=f32), 'ep')  209 us
    all_to_all x8, starting transfers between devices, exchange(): return lax.all_to_all(rows, 'ep', 0, 0, tiled=True)  130 us
  transfers between devices with their start and end apart: 9, of which 7 were waited for; matrix products, arithmetic and copies ran while one was open for 23% of the time, Pallas kernels for 0%

profile of v1, /device:TPU:0, one launch (start us, length us, event | category | flops | bytes accessed | tf_op | source)
XLA Modules:
  0.0 2718.1 jit_solution(12437551539325930964)
XLA Ops:
  10.2 23.0 scatter_custom_fusion
  35.3 16.1 gather_fusion.1
  51.5 7.5 all-to-all-start.2
  58.9 16.1 gather_fusion
  75.0 279.3 %all-to-all-done.2 = bf16[32,144,1536]{2,1,0:T(8,128)(2,1)} async-done(((bf16[32,144,1536]{2,1,0:T(8,128)(2,1)}), bf16[32,144,1536]{2,1,0:T(8,128)(2,1)}, u32[]{:S(2)}, u32[]{:S(2)}) %all-to-all-start.2) | async-done | bytes 14155808 | tf_op jit(solution)/shard_map/all_to_all | solution.py:44
  354.3 16.5 all-to-all-start
  378.3 7.7 pad.9
  386.1 37.2 %gather_fusion.3 = bf16[4608,1536]{1,0:T(8,128)(2,1)} fusion(bf16[6160,1536]{1,0:T(8,128)(2,1)} %pad.9, s32[5120]{0:T(1024)S(1)} %get-tuple-element.57), kind=kCustom, calls=%fused_computation.3 | custom fusion | bytes 28329984 | tf_op jit(solution)/shard_map/gather | solution.py:17
  423.2 242.7 %all-to-all-done = bf16[32,144,1536]{2,1,0:T(8,128)(2,1)} async-done(((bf16[32,144,1536]{2,1,0:T(8,128)(2,1)}), bf16[32,144,1536]{2,1,0:T(8,128)(2,1)}, u32[]{:S(2)}, u32[]{:S(2)}) %all-to-all-start) | async-done | bytes 14155808 | tf_op jit(solution)/shard_map/all_to_all | solution.py:44
  665.9 17.7 all-to-all-start.4
  683.6 37.1 %gather_fusion.5 = bf16[4608,1536]{1,0:T(8,128)(2,1)} fusion(bf16[6160,1536]{1,0:T(8,128)(2,1)} %pad.9, s32[5120]{0:T(1024)S(1)} %get-tuple-element.56), kind=kCustom, calls=%fused_computation.5 | custom fusion | bytes 28329984 | tf_op jit(solution)/shard_map/gather | solution.py:17
  720.7 256.9 %all-to-all-done.4 = bf16[32,144,1536]{2,1,0:T(8,128)(2,1)} async-done(((bf16[32,144,1536]{2,1,0:T(8,128)(2,1)}), bf16[32,144,1536]{2,1,0:T(8,128)(2,1)}, u32[]{:S(2)}, u32[]{:S(2)}) %all-to-all-start.4) | async-done | bytes 14155808 | tf_op jit(solution)/shard_map/all_to_all | solution.py:44
  977.7 18.5 all-to-all-start.6
  1003.0 21.5 convolution_add_fusion.1
  1024.6 23.2 fusion.7
  1049.9 10.5 add_convert_fusion.1
  1060.4 231.1 %all-to-all-done.6 = bf16[32,144,1536]{2,1,0:T(8,128)(2,1)} async-done(((bf16[32,144,1536]{2,1,0:T(8,128)(2,1)}), bf16[32,144,1536]{2,1,0:T(8,128)(2,1)}, u32[]{:S(2)}, u32[]{:S(2)}) %all-to-all-start.6) | async-done | bytes 14155808 | tf_op jit(solution)/shard_map/all_to_all | solution.py:44
  1291.5 17.3 all-to-all-start.1
  1309.4 5.6 convolution_convert_fusion.4
  1315.1 21.5 convolution_add_fusion
  1336.6 23.1 fusion.12
  1362.0 10.6 add_convert_fusion
  1372.6 231.6 %all-to-all-done.1 = bf16[32,144,1536]{2,1,0:T(8,128)(2,1)} async-done(((bf16[32,144,1536]{2,1,0:T(8,128)(2,1)}), bf16[32,144,1536]{2,1,0:T(8,128)(2,1)}, u32[]{:S(2)}, u32[]{:S(2)}) %all-to-all-start.1) | async-done | bytes 14155808 | tf_op jit(solution)/shard_map/all_to_all | solution.py:44
  1604.2 17.6 all-to-all-start.3
  1621.8 21.4 convolution_convert_fusion.1
  1643.2 273.9 %all-to-all-done.3 = bf16[32,144,1536]{2,1,0:T(8,128)(2,1)} async-done(((bf16[32,144,1536]{2,1,0:T(8,128)(2,1)}), bf16[32,144,1536]{2,1,0:T(8,128)(2,1)}, u32[]{:S(2)}, u32[]{:S(2)}) %all-to-all-start.3) | async-done | bytes 14155808 | tf_op jit(solution)/shard_map/all_to_all | solution.py:44
  1917.2 17.0 all-to-all-start.5
  1934.3 7.7 pad_maximum_fusion.3
  1942.0 28.9 %pad_maximum_fusion = bf16[9216,1536]{1,0:T(8,128)(2,1)} fusion(bf16[4608,1536]{1,0:T(8,128)(2,1)} %bitcast.14, bf16[4608,1536]{1,0:T(8,128)(2,1)} %bitcast.8), kind=kLoop, calls=%fused_computation.16 | loop fusion | flops 56623104 | bytes 56623104 | tf_op jit(solution)/shard_map/concatenate | solution.py:77
  1970.9 50.0 %gather_fusion.2 = bf16[6144,1536]{1,0:T(8,128)(2,1)} fusion(bf16[9216,1536]{1,0:T(8,128)(2,1)} %pad_maximum_fusion, s32[6144]{0:T(1024)S(1)} %broadcast_clamp_fusion.2), kind=kCustom, calls=%fused_computation.2 | custom fusion | bytes 37773312 | tf_op jit(solution)/shard_map/gather | solution.py:17
  2020.9 17.1 fusion.1
  2038.2 17.7 convolution_convert_fusion
  2055.9 173.2 %all-to-all-done.5 = bf16[32,144,1536]{2,1,0:T(8,128)(2,1)} async-done(((bf16[32,144,1536]{2,1,0:T(8,128)(2,1)}), bf16[32,144,1536]{2,1,0:T(8,128)(2,1)}, u32[]{:S(2)}, u32[]{:S(2)}) %all-to-all-start.5) | async-done | bytes 14155808 | tf_op jit(solution)/shard_map/all_to_all | solution.py:44
  2229.1 17.6 all-to-all-start.7
  2247.5 7.3 convert_reduce_fusion.2
  2254.8 7.3 convert_reduce_fusion.3
  2262.7 11.9 convolution_bitcast_fusion.3
  2274.7 11.7 convolution_bitcast_fusion.2
  2289.6 15.1 convert_reduce_fusion.5
  2304.7 21.8 convolution_bitcast_fusion.1
  2327.9 44.2 %gather_fusion.4 = bf16[6144,1536]{1,0:T(8,128)(2,1)} fusion(bf16[4608,1536]{1,0:T(8,128)(2,1)} %bitcast.23, s32[6144]{0:T(1024)S(1)} %broadcast_clamp_fusion.1), kind=kCustom, calls=%fused_computation.4 | custom fusion | bytes 37773312 | tf_op jit(solution)/shard_map/gather | solution.py:17
  2372.2 209.0 %psum.15 = f32[64]{0:T(128)} all-reduce(f32[64]{0:T(128)S(1)} %convert_reduce_fusion.6), channel_id=1, replica_groups=mesh['ep'=32] {'ep'}, use_global_device_ids=true, to_apply=%region_12.14 | all-reduce | flops 64 | bytes 512 | tf_op jit(solution)/shard_map/psum | solution.py:84
  2581.2 14.5 convert_reduce_fusion.4
  2596.3 19.1 convolution_bitcast_fusion
  2615.4 9.6 pad_maximum_fusion.1
  2625.1 13.9 convert_reduce_fusion.1
  2638.9 44.3 %gather_fusion.6 = bf16[6144,1536]{1,0:T(8,128)(2,1)} fusion(bf16[4608,1536]{1,0:T(8,128)(2,1)} %bitcast.29, s32[6144]{0:T(1024)S(1)} %copy-done.18), kind=kCustom, calls=%fused_computation.6 | custom fusion | bytes 37773312 | tf_op jit(solution)/shard_map/gather | solution.py:17
  2683.3 23.3 convert_reduce_fusion
  (136 shorter events, 35.7 us)
Async XLA Ops:
  7.2 363.7 %copy-start = (bf16[1536,64]{0,1:T(8,128)(2,1)S(1)}, bf16[1536,64]{0,1:T(8,128)(2,1)}, u32[]{:S(2)}) copy-start(bf16[1536,64]{0,1:T(8,128)(2,1)} %param.15) | copy-start | bytes 589828
  8.7 1.5 copy-start.19
  51.5 302.8 %all-to-all-start.2 = ((bf16[32,144,1536]{2,1,0:T(8,128)(2,1)}), bf16[32,144,1536]{2,1,0:T(8,128)(2,1)}, u32[]{:S(2)}, u32[]{:S(2)}) async-start(bf16[32,144,1536]{2,1,0:T(8,128)(2,1)} %bitcast.131), calls=%async_computation.2 | async-start | bytes 28311552 | tf_op jit(solution)/shard_map/all_to_all | solution.py:44
  354.3 16.6 copy-start.2
  354.3 16.6 copy-start.28
  354.3 17.6 copy-start.9
  354.3 311.6 %all-to-all-start = ((bf16[32,144,1536]{2,1,0:T(8,128)(2,1)}), bf16[32,144,1536]{2,1,0:T(8,128)(2,1)}, u32[]{:S(2)}, u32[]{:S(2)}) async-start(bf16[32,144,1536]{2,1,0:T(8,128)(2,1)} %bitcast.128), calls=%async_computation | async-start | bytes 28311552 | tf_op jit(solution)/shard_map/all_to_all | solution.py:44
  372.1 6.1 copy-start.7
  372.2 6.1 copy-start.11
  375.0 3.3 copy-start.1
  375.0 3.3 copy-start.16
  665.9 311.8 %all-to-all-start.4 = ((bf16[32,144,1536]{2,1,0:T(8,128)(2,1)}), bf16[32,144,1536]{2,1,0:T(8,128)(2,1)}, u32[]{:S(2)}, u32[]{:S(2)}) async-start(bf16[32,144,1536]{2,1,0:T(8,128)(2,1)} %bitcast.130), calls=%async_computation.4 | async-start | bytes 28311552 | tf_op jit(solution)/shard_map/all_to_all | solution.py:44
  977.6 18.5 copy-start.25
  977.6 19.1 copy-start.23
  977.7 313.9 %all-to-all-start.6 = ((bf16[32,144,1536]{2,1,0:T(8,128)(2,1)}), bf16[32,144,1536]{2,1,0:T(8,128)(2,1)}, u32[]{:S(2)}, u32[]{:S(2)}) async-start(bf16[32,144,1536]{2,1,0:T(8,128)(2,1)} %bitcast.129), calls=%async_computation.6 | async-start | bytes 28311552 | tf_op jit(solution)/shard_map/all_to_all | solution.py:44
  996.4 313.0 %copy-start.26 = (s32[1024]{0:T(1024)}, s32[1024]{0:T(1024)S(1)}, u32[]{:S(2)}) copy-start(s32[1024]{0:T(1024)S(1)} %fusion.51) | copy-start | bytes 12292
  1003.0 21.5 copy-start.33
  1003.0 21.5 copy-start.29
  1047.7 2.2 copy-start.35
  1291.5 312.7 %all-to-all-start.1 = ((bf16[32,144,1536]{2,1,0:T(8,128)(2,1)}), bf16[32,144,1536]{2,1,0:T(8,128)(2,1)}, u32[]{:S(2)}, u32[]{:S(2)}) async-start(bf16[32,144,1536]{2,1,0:T(8,128)(2,1)} %bitcast.134), calls=%async_computation.1 | async-start | bytes 28311552 | tf_op jit(solution)/shard_map/all_to_all | solution.py:44
  1315.0 21.5 copy-start.31
  1315.1 21.5 copy-start.30
  1336.6 25.4 copy-start.24
  1359.7 2.2 copy-start.36
  1604.2 17.6 copy-start.34
  1604.2 312.9 %all-to-all-start.3 = ((bf16[32,144,1536]{2,1,0:T(8,128)(2,1)}), bf16[32,144,1536]{2,1,0:T(8,128)(2,1)}, u32[]{:S(2)}, u32[]{:S(2)}) async-start(bf16[32,144,1536]{2,1,0:T(8,128)(2,1)} %bitcast.135), calls=%async_computation.3 | async-start | bytes 28311552 | tf_op jit(solution)/shard_map/all_to_all | solution.py:44
  1917.1 17.0 copy-start.15
  1917.1 17.1 copy-start.8
  1917.2 17.1 copy-start.12
  1917.2 17.1 copy-start.17
  1917.2 311.9 %all-to-all-start.5 = ((bf16[32,144,1536]{2,1,0:T(8,128)(2,1)}), bf16[32,144,1536]{2,1,0:T(8,128)(2,1)}, u32[]{:S(2)}, u32[]{:S(2)}) async-start(bf16[32,144,1536]{2,1,0:T(8,128)(2,1)} %bitcast.133), calls=%async_computation.5 | async-start | bytes 28311552 | tf_op jit(solution)/shard_map/all_to_all | solution.py:44
  1970.8 50.0 %copy-start.20 = (pred[6,1024]{1,0:T(8,128)(4,1)S(1)}, pred[6,1024]{1,0:T(8,128)(4,1)}, u32[]{:S(2)}) copy-start(pred[6,1024]{1,0:T(8,128)(4,1)} %copy-done.19) | copy-start | bytes 18436
  2020.9 17.1 copy-start.10
  2020.9 17.3 copy-start.5
  2020.9 17.3 copy-start.32
  2229.1 17.6 copy-start.13
  2229.1 17.7 copy-start.14
  2229.1 409.9 %all-to-all-start.7 = ((bf16[32,144,1536]{2,1,0:T(8,128)(2,1)}), bf16[32,144,1536]{2,1,0:T(8,128)(2,1)}, u32[]{:S(2)}, u32[]{:S(2)}) async-start(bf16[32,144,1536]{2,1,0:T(8,128)(2,1)} %bitcast.132), calls=%async_computation.7 | async-start | bytes 28311552 | tf_op jit(solution)/shard_map/all_to_all | solution.py:44
  2246.6 462.7 %all-reduce.4.cloned.1.call-start = ((), (), s32[]{:S(2)}) async-start(), calls=%async_computation.8 | async-start | bytes 786432 | tf_op jit(solution)/shard_map/psum | solution.py:83
  2262.7 26.8 slice-start
  2274.7 14.9 slice-start.1
  2286.4 3.2 copy-start.27
  2304.7 21.8 copy-start.3
  2596.3 19.1 copy-start.6
  2615.4 9.6 copy-start.22
  2625.1 13.9 copy-start.18
  2638.9 44.4 %copy-start.21 = (pred[6,1024]{1,0:T(8,128)(4,1)S(1)}, pred[6,1024]{1,0:T(8,128)(4,1)}, u32[]{:S(2)}) copy-start(pred[6,1024]{1,0:T(8,128)(4,1)} %get-tuple-element.37) | copy-start | bytes 18436
  2683.3 23.3 copy-start.4
Sparse Core Ops, SparseCore 0:
  2328.0 188.5 all-reduce.3
